TPU v7x, 128 devices: a whole 4x4x4 slice. The times are simulated.
128 devices in a mesh: col: 32 (over z, y, x_hi), row: 4 (over x_lo, core).
Axes of the slice: x: 4 (x_hi: 2, x_lo: 2; x = x_hi * 2 + x_lo), y: 4, z: 4, core: 2. Of those that a mesh axis runs over, the one named last changes fastest.
Arguments:
- hamiltonian: float32 [16384, 16384], P('row', 'col'), as said below
Outputs:
- reduced: float32 [16384, 16384], P('row', 'col')
Inputs may be any that keep to these rules, and one draw needn't show every extreme that they name: hamiltonian is symmetric.
All inputs are finite; a program needn't handle non-finite values.
Results may differ from a plain program's by a relative error of at most 0.00019.
Values sent between devices are 32-bit elements; how exact they have to be, the bound alone decides.
No kernel may reach another device: no remote copies, remote signals or barrier semaphores. Data moves between devices by JAX's collectives and lax.ppermute only.
A program may use at most 128 MiB of HBM per device.

v0:
```python
import jax
import jax.numpy as jnp
from jax import lax
from jax.sharding import PartitionSpec as P

NB = 256
PANELS = 2


def from_root(block, axis, holder):
    block = jnp.where(lax.axis_index(axis) == holder, block, jnp.zeros_like(block))
    return lax.psum(block, axis)


def product(left, right):
    return jnp.dot(left, right, precision=lax.Precision.HIGHEST, preferred_element_type=jnp.float32)


def inner_tn(left, right):
    return lax.dot_general(
        left,
        right,
        (((0,), (0,)), ((), ())),
        precision=lax.Precision.HIGHEST,
        preferred_element_type=jnp.float32,
    )


def outer_nt(left, right):
    return lax.dot_general(
        left,
        right,
        (((1,), (1,)), ((), ())),
        precision=lax.Precision.HIGHEST,
        preferred_element_type=jnp.float32,
    )


def solve_right(gram, panel):
    lower = jnp.linalg.cholesky(gram)
    return lax.linalg.triangular_solve(lower, panel, left_side=False, lower=True, transpose_a=True)


def coupling_of(top_rows):
    square = jnp.eye(NB, dtype=jnp.float32) - top_rows.T
    normal_eq = inner_tn(square, square)
    factor = jnp.linalg.cholesky(normal_eq)
    middle = lax.linalg.triangular_solve(factor, square.T, left_side=True, lower=True)
    return lax.linalg.triangular_solve(factor, middle, left_side=True, lower=True, transpose_a=True)


def shards(hamiltonian):
    matrix = hamiltonian
    row_block = matrix.shape[0]
    col_block = matrix.shape[1]
    ratio = lax.axis_size("col") // lax.axis_size("row")
    row_pos = lax.axis_index("row")
    col_pos = lax.axis_index("col")
    global_rows = row_pos * row_block + jnp.arange(row_block, dtype=jnp.int32)
    owner = col_pos // ratio
    offset = col_pos % ratio * col_block
    for panel_index in range(PANELS):
        first_col = panel_index * NB
        first_row = first_col + NB
        live = (global_rows >= first_row)[:, None]
        panel = jnp.where(live, matrix[:, first_col : first_col + NB], jnp.float32(0.0))
        gram = lax.psum(inner_tn(panel, panel), "row")
        basis = solve_right(gram, panel)
        top_rows = from_root(basis[first_row : first_row + NB], "row", 0)
        coupling = coupling_of(top_rows)
        ident = (
            global_rows[:, None] - first_row == jnp.arange(NB, dtype=jnp.int32)[None, :]
        ).astype(jnp.float32)
        vectors = ident - basis
        vectors, coupling = (from_root(vectors, "col", 0), from_root(coupling, "col", 0))
        column_vectors = from_root(
            lax.dynamic_slice_in_dim(vectors, offset, col_block, 0), "row", owner
        )
        applied = lax.psum(product(matrix, column_vectors), "col")
        applied = product(applied, coupling)
        inner = lax.psum(inner_tn(vectors, applied), "row")
        inner = product(coupling.T, inner)
        shifted = applied - 0.5 * product(vectors, inner)
        column_shifted = from_root(
            lax.dynamic_slice_in_dim(shifted, offset, col_block, 0), "row", owner
        )
        matrix = matrix - outer_nt(vectors, column_shifted) - outer_nt(shifted, column_vectors)
    return matrix


def solution(mesh):
    return jax.shard_map(
        shards, mesh=mesh, in_specs=(P("row", "col"),), out_specs=P("row", "col"), check_vma=False
    )
```

profile of v0, /device:TPU:1, one launch (start us, length us, event | category | flops | bytes accessed | tf_op | source)
XLA Modules:
  0.0 2289.1 jit_solution(8985189598274994049)
XLA Ops:
  24.4 39.6 %all-reduce.18.cloned.1.call-done = f32[256,256]{0,1:T(8,128)} async-done(((f32[256,256]{0,1:T(8,128)}), f32[256,256]{0,1:T(8,128)}) %all-reduce.18.cloned.1.call-update) | async-done | bytes 262160 | tf_op jit(solution)/shard_map/psum | solution.py:67
  66.1 11.7 cholesky.214
  88.2 11.7 cholesky.231
  106.4 19.7 custom-call.24
  139.4 357.7 %all-reduce.20.cloned.1.call-done = f32[4096,256]{0,1:T(8,128)} async-done(((f32[4096,256]{0,1:T(8,128)}), f32[4096,256]{0,1:T(8,128)}) %all-reduce.20.cloned.1.call-update) | async-done | bytes 4194320 | tf_op jit(solution)/shard_map/psum | solution.py:12
  499.5 60.5 %all-reduce.40.cloned.1.call-done = (f32[512,256]{0,1:T(8,128)}, f32[256,256]{0,1:T(8,128)}) async-done(((f32[512,256]{0,1:T(8,128)}, f32[256,256]{0,1:T(8,128)}), (f32[512,256]{0,1:T(8,128)}, f32[256,256]{0,1:T(8,128)})) %all-reduce.40.cloned.1.call-update) | async-done | bytes 786448 | tf_op jit(solution)/shard_map/psum | solution.py:12
  562.9 11.7 cholesky.248
  585.0 11.7 cholesky.265
  603.5 19.7 custom-call.27
  637.0 362.5 %all-reduce.36.cloned.1.call-done = (f32[4096,256]{0,1:T(8,128)}, f32[256,256]{0,1:T(8,128)}) async-done(((f32[4096,256]{0,1:T(8,128)}, f32[256,256]{0,1:T(8,128)}), (f32[4096,256]{0,1:T(8,128)}, f32[256,256]{0,1:T(8,128)})) %all-reduce.36.cloned.1.call-update) | async-done | bytes 4456464 | tf_op jit(solution)/shard_map/psum | solution.py:79
  1020.5 50.7 %all-reduce.22.cloned.1.call-done = f32[256,256]{1,0:T(8,128)} async-done(((f32[256,256]{1,0:T(8,128)}), f32[256,256]{1,0:T(8,128)}) %all-reduce.22.cloned.1.call-update) | async-done | bytes 262160 | tf_op jit(solution)/shard_map/psum | solution.py:81
  1083.5 38.6 %all-reduce.24.cloned.1.call-done = f32[512,256]{0,1:T(8,128)} async-done(((f32[512,256]{0,1:T(8,128)}), f32[512,256]{0,1:T(8,128)}) %all-reduce.24.cloned.1.call-update) | async-done | bytes 524304 | tf_op jit(solution)/shard_map/psum | solution.py:12
  1153.1 36.9 %all-reduce.26.cloned.1.call-done = f32[256,256]{0,1:T(8,128)} async-done(((f32[256,256]{0,1:T(8,128)}), f32[256,256]{0,1:T(8,128)}) %all-reduce.26.cloned.1.call-update) | async-done | bytes 262160 | tf_op jit(solution)/shard_map/psum | solution.py:67
  1214.1 11.7 cholesky.299
  1232.9 19.7 custom-call.29
  1265.9 357.7 %all-reduce.28.cloned.1.call-done = f32[4096,256]{0,1:T(8,128)} async-done(((f32[4096,256]{0,1:T(8,128)}), f32[4096,256]{0,1:T(8,128)}) %all-reduce.28.cloned.1.call-update) | async-done | bytes 4194320 | tf_op jit(solution)/shard_map/psum | solution.py:12
  1626.1 60.3 %all-reduce.38.cloned.1.call-done = (f32[512,256]{0,1:T(8,128)}, f32[256,256]{0,1:T(8,128)}) async-done(((f32[512,256]{0,1:T(8,128)}, f32[256,256]{0,1:T(8,128)}), (f32[512,256]{0,1:T(8,128)}, f32[256,256]{0,1:T(8,128)})) %all-reduce.38.cloned.1.call-update) | async-done | bytes 786448 | tf_op jit(solution)/shard_map/psum | solution.py:12
  1711.3 11.7 cholesky.333
  1730.2 19.7 custom-call.32
  1752.0 16.9 fusion.66
  1769.7 362.3 %all-reduce.34.cloned.1.call-done = (f32[4096,256]{1,0:T(8,128)}, f32[256,256]{0,1:T(8,128)}) async-done(((f32[4096,256]{1,0:T(8,128)}, f32[256,256]{0,1:T(8,128)}), (f32[4096,256]{1,0:T(8,128)}, f32[256,256]{0,1:T(8,128)})) %all-reduce.34.cloned.1.call-update) | async-done | bytes 4456464 | tf_op jit(solution)/shard_map/psum | solution.py:79
  2149.8 50.4 %all-reduce.30.cloned.1.call-done = f32[256,256]{1,0:T(8,128)} async-done(((f32[256,256]{1,0:T(8,128)}), f32[256,256]{1,0:T(8,128)}) %all-reduce.30.cloned.1.call-update) | async-done | bytes 262160 | tf_op jit(solution)/shard_map/psum | solution.py:81
  2212.4 38.7 %all-reduce.32.cloned.1.call-done = f32[512,256]{0,1:T(8,128)} async-done(((f32[512,256]{0,1:T(8,128)}), f32[512,256]{0,1:T(8,128)}) %all-reduce.32.cloned.1.call-update) | async-done | bytes 524304 | tf_op jit(solution)/shard_map/psum | solution.py:12
  2260.7 12.4 subtract_subtract_fusion
  (203 shorter events, 291.1 us)
Async XLA Ops:
  6.5 57.5 %all-reduce.18.cloned.1.call-start = ((), (), s32[]{:S(2)}) async-start(), calls=%async_computation | async-start | bytes 524288 | tf_op jit(solution)/shard_map/psum | solution.py:67
  24.1 473.0 %all-reduce.20.cloned.1.call-start = ((), (), s32[]{:S(2)}) async-start(), calls=%async_computation.1 | async-start | bytes 8388608 | tf_op jit(solution)/shard_map/psum | solution.py:12
  126.0 3.7 copy-start.2
  137.6 422.4 %all-reduce.40.cloned.1.call-start = ((), (), s32[]{:S(2)}) async-start(), calls=%async_computation.11 | async-start | bytes 1572864 | tf_op jit(solution)/shard_map/psum | solution.py:12
  499.1 500.5 %all-reduce.36.cloned.1.call-start = ((), (), s32[]{:S(2)}) async-start(), calls=%async_computation.9 | async-start | bytes 8912896 | tf_op jit(solution)/shard_map/psum | solution.py:79
  560.0 65.3 %copy-start.16 = (f32[512,256]{0,1:T(8,128)S(1)}, f32[512,256]{0,1:T(8,128)}, u32[]{:S(2)}) copy-start(f32[512,256]{0,1:T(8,128)} %get-tuple-element.95) | copy-start | bytes 1572868
  637.0 434.2 %all-reduce.22.cloned.1.call-start = ((), (), s32[]{:S(2)}) async-start(), calls=%async_computation.2 | async-start | bytes 524288 | tf_op jit(solution)/shard_map/psum | solution.py:81
  999.5 10.8 copy-start.5
  1008.4 2.0 copy-start.7
  1014.7 56.5 %copy-start.17 = (f32[256,256]{0,1:T(8,128)S(1)}, f32[256,256]{0,1:T(8,128)}, u32[]{:S(2)}) copy-start(f32[256,256]{0,1:T(8,128)} %get-tuple-element.92) | copy-start | bytes 786436
  1014.7 107.5 %all-reduce.24.cloned.1.call-start = ((), (), s32[]{:S(2)}) async-start(), calls=%async_computation.3 | async-start | bytes 1048576 | tf_op jit(solution)/shard_map/psum | solution.py:12
  1083.5 106.5 %all-reduce.26.cloned.1.call-start = ((), (), s32[]{:S(2)}) async-start(), calls=%async_computation.4 | async-start | bytes 524288 | tf_op jit(solution)/shard_map/psum | solution.py:67
  1122.2 10.1 copy-start.10
  1143.3 3.4 copy-start
  1152.9 470.8 %all-reduce.28.cloned.1.call-start = ((), (), s32[]{:S(2)}) async-start(), calls=%async_computation.5 | async-start | bytes 8388608 | tf_op jit(solution)/shard_map/psum | solution.py:12
  1252.6 3.7 copy-start.4
  1264.2 422.2 %all-reduce.38.cloned.1.call-start = ((), (), s32[]{:S(2)}) async-start(), calls=%async_computation.10 | async-start | bytes 1572864 | tf_op jit(solution)/shard_map/psum | solution.py:12
  1625.6 506.5 %all-reduce.34.cloned.1.call-start = ((), (), s32[]{:S(2)}) async-start(), calls=%async_computation.8 | async-start | bytes 8912896 | tf_op jit(solution)/shard_map/psum | solution.py:79
  1686.4 65.6 %copy-start.15 = (f32[512,256]{0,1:T(8,128)S(1)}, f32[512,256]{0,1:T(8,128)}, u32[]{:S(2)}) copy-start(f32[512,256]{0,1:T(8,128)} %get-tuple-element.93) | copy-start | bytes 1572868
  1769.6 430.5 %all-reduce.30.cloned.1.call-start = ((), (), s32[]{:S(2)}) async-start(), calls=%async_computation.6 | async-start | bytes 524288 | tf_op jit(solution)/shard_map/psum | solution.py:81
  2132.0 7.4 copy-start.6
  2143.8 56.3 %copy-start.18 = (f32[256,256]{0,1:T(8,128)S(1)}, f32[256,256]{0,1:T(8,128)}, u32[]{:S(2)}) copy-start(f32[256,256]{0,1:T(8,128)} %get-tuple-element.90) | copy-start | bytes 786436
  2143.8 107.3 %all-reduce.32.cloned.1.call-start = ((), (), s32[]{:S(2)}) async-start(), calls=%async_computation.7 | async-start | bytes 1048576 | tf_op jit(solution)/shard_map/psum | solution.py:12
  2251.1 9.6 copy-start.12
  (7 other events, 12.6 us)
Sparse Core Ops, SparseCore 0:
  24.3 39.6 all-reduce.17
  137.8 359.3 all-reduce.19
  499.9 60.0 all-reduce.39
  637.1 362.3 all-reduce.35
  1014.8 56.3 all-reduce.21
  1083.6 38.5 all-reduce.23
  1153.0 36.9 all-reduce.25
  1264.3 359.2 all-reduce.27
  1626.2 60.0 all-reduce.37
  1769.8 362.2 all-reduce.33
  2143.9 56.1 all-reduce.29
  2212.5 38.5 all-reduce.31
where the time goes:
time: 2290 us
  waiting for transfers between devices  1820 us (79%)
  other arithmetic  239 us (10%)
  matrix products  145 us (6%)
  local copies, waits for them, and re-layouts  65.9 us (3%)
    psum x6, waiting for transfers between devices, from_root(): return lax.psum(block, axis)  914 us
    psum x2, waiting for transfers between devices, shards(): applied = lax.psum(product(matrix, column_vectors), 'col')  725 us
    psum x2, waiting for transfers between devices, shards(): inner = lax.psum(inner_tn(vectors, applied), 'row')  101 us
    psum x2, waiting for transfers between devices, shards(): gram = lax.psum(inner_tn(panel, panel), 'row')  76.5 us
    another operation x14, other arithmetic, coupling_of(): factor = jnp.linalg.cholesky(normal_eq)  69.4 us
    another operation x13, other arithmetic, solve_right(): lower = jnp.linalg.cholesky(gram)  68.7 us
    dot_general x8, matrix products, product(): jnp.dot(left, right, precision=lax.Precision.HIGHEST, preferred_element_t...  60.7 us
  transfers between devices with their start and end apart: 12, of which 12 were waited for; matrix products, arithmetic and copies ran while one was open for 1% of the time, Pallas kernels for 0%

commit v1 on v0

--- a/solution.py
+++ b/solution.py
@@ -78,7 +78,11 @@
         )
         applied = lax.psum(product(matrix, column_vectors), "col")
         applied = product(applied, coupling)
-        inner = lax.psum(inner_tn(vectors, applied), "row")
+
+        def reach_the_spots(field):
+            return jnp.sum(jax.lax.all_gather(field, "row"), axis=0)
+
+        inner = reach_the_spots(inner_tn(vectors, applied))
         inner = product(coupling.T, inner)
         shifted = applied - 0.5 * product(vectors, inner)
         column_shifted = from_root(

time: 2290 us -> 2260 us (0.987)
  waiting for transfers between devices: 1820 us -> 1790 us
    psum x2 -> x0, waiting for transfers between devices: 101 us -> none  [shards(): inner = lax.psum(inner_tn(vectors, applied), 'row')]
    all_gather x0 -> x2, waiting for transfers between devices: none -> 70.1 us  [reach_the_spots(): return jnp.sum(jax.lax.all_gather(field, 'row'), axis=0)]
where the time goes in v1:
time: 2260 us
  waiting for transfers between devices  1790 us (79%)
  other arithmetic  242 us (11%)
  matrix products  143 us (6%)
  local copies, waits for them, and re-layouts  65.9 us (3%)
    psum x6, waiting for transfers between devices, from_root(): return lax.psum(block, axis)  914 us
    psum x2, waiting for transfers between devices, shards(): applied = lax.psum(product(matrix, column_vectors), 'col')  725 us
    psum x2, waiting for transfers between devices, shards(): gram = lax.psum(inner_tn(panel, panel), 'row')  76.5 us
    all_gather x2, waiting for transfers between devices, reach_the_spots(): return jnp.sum(jax.lax.all_gather(field, 'row'), axis=0)  70.1 us
    another operation x14, other arithmetic, coupling_of(): factor = jnp.linalg.cholesky(normal_eq)  69.4 us
    another operation x13, other arithmetic, solve_right(): lower = jnp.linalg.cholesky(gram)  68.7 us
    dot_general x8, matrix products, product(): jnp.dot(left, right, precision=lax.Precision.HIGHEST, preferred_element_t...  58.9 us
  transfers between devices with their start and end apart: 12, of which 12 were waited for; matrix products, arithmetic and copies ran while one was open for 1% of the time, Pallas kernels for 0%

profile of v1, /device:TPU:1, one launch (start us, length us, event | category | flops | bytes accessed | tf_op | source)
XLA Modules:
  0.0 2259.3 jit_solution(15180738569823051124)
XLA Ops:
  24.4 39.6 %all-reduce.16.cloned.1.call-done = f32[256,256]{0,1:T(8,128)} async-done(((f32[256,256]{0,1:T(8,128)}), f32[256,256]{0,1:T(8,128)}) %all-reduce.16.cloned.1.call-update) | async-done | bytes 262160 | tf_op jit(solution)/shard_map/psum | solution.py:67
  66.1 11.7 cholesky.214
  88.2 11.7 cholesky.231
  106.4 19.7 custom-call.24
  139.4 357.7 %all-reduce.18.cloned.1.call-done = f32[4096,256]{0,1:T(8,128)} async-done(((f32[4096,256]{0,1:T(8,128)}), f32[4096,256]{0,1:T(8,128)}) %all-reduce.18.cloned.1.call-update) | async-done | bytes 4194320 | tf_op jit(solution)/shard_map/psum | solution.py:12
  499.5 60.5 %all-reduce.34.cloned.1.call-done = (f32[512,256]{0,1:T(8,128)}, f32[256,256]{0,1:T(8,128)}) async-done(((f32[512,256]{0,1:T(8,128)}, f32[256,256]{0,1:T(8,128)}), (f32[512,256]{0,1:T(8,128)}, f32[256,256]{0,1:T(8,128)})) %all-reduce.34.cloned.1.call-update) | async-done | bytes 786448 | tf_op jit(solution)/shard_map/psum | solution.py:12
  562.9 11.7 cholesky.248
  585.0 11.7 cholesky.265
  603.5 19.7 custom-call.27
  637.0 362.5 %all-reduce.30.cloned.1.call-done = (f32[4096,256]{0,1:T(8,128)}, f32[256,256]{0,1:T(8,128)}) async-done(((f32[4096,256]{0,1:T(8,128)}, f32[256,256]{0,1:T(8,128)}), (f32[4096,256]{0,1:T(8,128)}, f32[256,256]{0,1:T(8,128)})) %all-reduce.30.cloned.1.call-update) | async-done | bytes 4456464 | tf_op jit(solution)/shard_map/psum | solution.py:79
  1020.4 35.1 %all-gather.5.cloned.1.call-done = f32[1024,256]{1,0:T(8,128)} async-done(((f32[256,256]{1,0:T(8,128)}), f32[1024,256]{1,0:T(8,128)}) %all-gather.5.cloned.1.call-update) | async-done | bytes 1048592 | tf_op jit(solution)/shard_map/all_gather | solution.py:83
  1068.3 38.6 %all-reduce.20.cloned.1.call-done = f32[512,256]{0,1:T(8,128)} async-done(((f32[512,256]{0,1:T(8,128)}), f32[512,256]{0,1:T(8,128)}) %all-reduce.20.cloned.1.call-update) | async-done | bytes 524304 | tf_op jit(solution)/shard_map/psum | solution.py:12
  1137.8 36.9 %all-reduce.22.cloned.1.call-done = f32[256,256]{0,1:T(8,128)} async-done(((f32[256,256]{0,1:T(8,128)}), f32[256,256]{0,1:T(8,128)}) %all-reduce.22.cloned.1.call-update) | async-done | bytes 262160 | tf_op jit(solution)/shard_map/psum | solution.py:67
  1198.8 11.7 cholesky.299
  1217.6 19.7 custom-call.29
  1250.6 357.8 %all-reduce.24.cloned.1.call-done = f32[4096,256]{0,1:T(8,128)} async-done(((f32[4096,256]{0,1:T(8,128)}), f32[4096,256]{0,1:T(8,128)}) %all-reduce.24.cloned.1.call-update) | async-done | bytes 4194320 | tf_op jit(solution)/shard_map/psum | solution.py:12
  1610.9 60.5 %all-reduce.32.cloned.1.call-done = (f32[512,256]{0,1:T(8,128)}, f32[256,256]{0,1:T(8,128)}) async-done(((f32[512,256]{0,1:T(8,128)}, f32[256,256]{0,1:T(8,128)}), (f32[512,256]{0,1:T(8,128)}, f32[256,256]{0,1:T(8,128)})) %all-reduce.32.cloned.1.call-update) | async-done | bytes 786448 | tf_op jit(solution)/shard_map/psum | solution.py:12
  1696.3 11.7 cholesky.333
  1715.2 19.7 custom-call.32
  1737.0 16.9 fusion.66
  1754.7 362.6 %all-reduce.28.cloned.1.call-done = (f32[4096,256]{1,0:T(8,128)}, f32[256,256]{0,1:T(8,128)}) async-done(((f32[4096,256]{1,0:T(8,128)}, f32[256,256]{0,1:T(8,128)}), (f32[4096,256]{1,0:T(8,128)}, f32[256,256]{0,1:T(8,128)})) %all-reduce.28.cloned.1.call-update) | async-done | bytes 4456464 | tf_op jit(solution)/shard_map/psum | solution.py:79
  2135.0 34.9 %all-gather.7.cloned.1.call-done = f32[1024,256]{1,0:T(8,128)} async-done(((f32[256,256]{1,0:T(8,128)}), f32[1024,256]{1,0:T(8,128)}) %all-gather.7.cloned.1.call-update) | async-done | bytes 1048592 | tf_op jit(solution)/shard_map/all_gather | solution.py:83
  2182.6 38.6 %all-reduce.26.cloned.1.call-done = f32[512,256]{0,1:T(8,128)} async-done(((f32[512,256]{0,1:T(8,128)}), f32[512,256]{0,1:T(8,128)}) %all-reduce.26.cloned.1.call-update) | async-done | bytes 524304 | tf_op jit(solution)/shard_map/psum | solution.py:12
  2230.9 12.4 subtract_subtract_fusion
  (205 shorter events, 291.8 us)
Async XLA Ops:
  6.5 57.5 %all-reduce.16.cloned.1.call-start = ((), (), s32[]{:S(2)}) async-start(), calls=%async_computation | async-start | bytes 524288 | tf_op jit(solution)/shard_map/psum | solution.py:67
  24.1 473.0 %all-reduce.18.cloned.1.call-start = ((), (), s32[]{:S(2)}) async-start(), calls=%async_computation.1 | async-start | bytes 8388608 | tf_op jit(solution)/shard_map/psum | solution.py:12
  126.0 3.7 copy-start.2
  137.6 422.4 %all-reduce.34.cloned.1.call-start = ((), (), s32[]{:S(2)}) async-start(), calls=%async_computation.11 | async-start | bytes 1572864 | tf_op jit(solution)/shard_map/psum | solution.py:12
  499.1 500.4 %all-reduce.30.cloned.1.call-start = ((), (), s32[]{:S(2)}) async-start(), calls=%async_computation.9 | async-start | bytes 8912896 | tf_op jit(solution)/shard_map/psum | solution.py:79
  560.0 65.3 %copy-start.16 = (f32[512,256]{0,1:T(8,128)S(1)}, f32[512,256]{0,1:T(8,128)}, u32[]{:S(2)}) copy-start(f32[512,256]{0,1:T(8,128)} %get-tuple-element.95) | copy-start | bytes 1572868
  637.0 418.6 %all-gather.5.cloned.1.call-start = ((), (), s32[]{:S(2)}) async-start(), calls=%async_computation.6 | async-start | bytes 1310720 | tf_op jit(solution)/shard_map/all_gather | solution.py:83
  999.5 10.8 copy-start.5
  1008.4 2.0 copy-start.7
  1014.7 42.2 %copy-start.18 = (f32[256,256]{0,1:T(8,128)S(1)}, f32[256,256]{0,1:T(8,128)}, u32[]{:S(2)}) copy-start(f32[256,256]{0,1:T(8,128)} %get-tuple-element.92) | copy-start | bytes 786436
  1014.7 92.2 %all-reduce.20.cloned.1.call-start = ((), (), s32[]{:S(2)}) async-start(), calls=%async_computation.2 | async-start | bytes 1048576 | tf_op jit(solution)/shard_map/psum | solution.py:12
  1068.2 106.5 %all-reduce.22.cloned.1.call-start = ((), (), s32[]{:S(2)}) async-start(), calls=%async_computation.3 | async-start | bytes 524288 | tf_op jit(solution)/shard_map/psum | solution.py:67
  1106.9 10.1 copy-start.10
  1128.0 3.4 copy-start
  1137.6 470.9 %all-reduce.24.cloned.1.call-start = ((), (), s32[]{:S(2)}) async-start(), calls=%async_computation.4 | async-start | bytes 8388608 | tf_op jit(solution)/shard_map/psum | solution.py:12
  1237.3 3.7 copy-start.4
  1248.9 422.5 %all-reduce.32.cloned.1.call-start = ((), (), s32[]{:S(2)}) async-start(), calls=%async_computation.10 | async-start | bytes 1572864 | tf_op jit(solution)/shard_map/psum | solution.py:12
  1610.4 506.9 %all-reduce.28.cloned.1.call-start = ((), (), s32[]{:S(2)}) async-start(), calls=%async_computation.8 | async-start | bytes 8912896 | tf_op jit(solution)/shard_map/psum | solution.py:79
  1671.4 65.6 %copy-start.15 = (f32[512,256]{0,1:T(8,128)S(1)}, f32[512,256]{0,1:T(8,128)}, u32[]{:S(2)}) copy-start(f32[512,256]{0,1:T(8,128)} %get-tuple-element.93) | copy-start | bytes 1572868
  1754.6 415.3 %all-gather.7.cloned.1.call-start = ((), (), s32[]{:S(2)}) async-start(), calls=%async_computation.7 | async-start | bytes 1310720 | tf_op jit(solution)/shard_map/all_gather | solution.py:83
  2117.3 7.4 copy-start.6
  2129.1 42.2 %copy-start.17 = (f32[256,256]{0,1:T(8,128)S(1)}, f32[256,256]{0,1:T(8,128)}, u32[]{:S(2)}) copy-start(f32[256,256]{0,1:T(8,128)} %get-tuple-element.90) | copy-start | bytes 786436
  2129.1 92.2 %all-reduce.26.cloned.1.call-start = ((), (), s32[]{:S(2)}) async-start(), calls=%async_computation.5 | async-start | bytes 1048576 | tf_op jit(solution)/shard_map/psum | solution.py:12
  2221.3 9.6 copy-start.12
  (7 other events, 12.6 us)
Sparse Core Ops, SparseCore 0:
  24.3 39.6 all-reduce.15
  137.8 359.3 all-reduce.17
  499.9 60.0 all-reduce.33
  637.1 362.3 all-reduce.29
  1014.8 40.7 all-gather.4
  1068.3 38.5 all-reduce.19
  1137.7 36.9 all-reduce.21
  1249.0 359.3 all-reduce.23
  1611.2 60.1 all-reduce.31
  1754.8 362.5 all-reduce.27
  2129.2 40.7 all-gather.6
  2182.7 38.4 all-reduce.25
